TPU v7x, 256 devices: a whole 4x4x8 slice. The times are simulated.
256 devices in a mesh: rows: 8 (over x, core), cols: 32 (over y, z).
Axes of the slice: x: 4, y: 4, z: 8, core: 2. Of those that a mesh axis runs over, the one named last changes fastest.
Arguments:
- features: bfloat16 [256, 4096, 1536], P('rows', 'cols'), may hold values from -6 to 6
- projection: bfloat16 [1536, 128], replicated, may hold values from -0.4375 to 0.4375
- prev_dist: float32 [256, 4096], P('rows', 'cols'), may hold values from 0.5 to 3
- valid: int32 [256, 4096], P('rows', 'cols'), may hold values 0 or 1
- pick_owner: int32 [512], replicated, may hold values from 0 to 255, as said below
- pick_slot: int32 [512], replicated, may hold values from 0 to 4095, as said below
Outputs:
- min_dist: float32 [256, 4096], P('rows', 'cols')
Inputs may be any that keep to these rules, and one draw needn't show every extreme that they name: `pick_owner`: no two picks name the same patch; picks fall on devices at random. `pick_slot`: see pick_owner.
All inputs are finite; a program needn't handle non-finite values. No bound on the sum of `valid` on one device may be relied on, other than what follows from the above.
Results may differ from a plain program's by a relative error of at most 0.0003.
Values may be sent and summed in bfloat16 or wider, within the bound.
A program may use at most 128 MiB of HBM per device.

v0:
```python
import jax
import jax.numpy as jnp
from jax import lax
from jax.sharding import PartitionSpec as P

D_PROJ = 128


def padded_2(block, sides, width):
    for axis, dim in sides:
        count = lax.axis_size(axis)
        forward = [(i, i + 1) for i in range(count - 1)]
        backward = [(target, source) for source, target in forward]
        low = lax.ppermute(
            lax.slice_in_dim(block, block.shape[dim] - width, None, axis=dim), axis, forward
        )
        high = lax.ppermute(lax.slice_in_dim(block, 0, width, axis=dim), axis, backward)
        block = jnp.concatenate([low, block, high], axis=dim)
    return block


def window_sum(padded, rows_dev, cols_dev):
    total = jnp.zeros((rows_dev, cols_dev, padded.shape[2]), jnp.float32)
    for row_off in range(3):
        for col_off in range(3):
            total = total + padded[
                row_off : row_off + rows_dev, col_off : col_off + cols_dev
            ].astype(jnp.float32)
    return total / 9.0


def shards(features, projection, prev_dist, valid, pick_owner, pick_slot):
    rows_dev, cols_dev, channels = features.shape
    proj_full = projection.astype(jnp.float32)
    own_index = lax.axis_index("rows") * lax.axis_size("cols") + lax.axis_index("cols")
    owned = pick_owner == own_index
    padded = padded_2(features, (("rows", 0), ("cols", 1)), 1)
    pooled = window_sum(padded, rows_dev, cols_dev).reshape(rows_dev * cols_dev, channels)
    projected = jnp.dot(pooled, proj_full, precision=lax.Precision.HIGHEST)
    local_rows = jnp.where(owned[:, None], projected[pick_slot], jnp.float32(0.0))
    pick_rows = lax.psum(local_rows, ("rows", "cols"))
    pick_sq = jnp.sum(pick_rows * pick_rows, axis=1)
    own_sq = jnp.sum(projected * projected, axis=1)
    inner_prod = jnp.dot(projected, pick_rows.T, precision=lax.Precision.HIGHEST)
    scaled_gap = (own_sq[:, None] + pick_sq[None, :] - 2.0 * inner_prod) / D_PROJ
    nearest = jnp.min(scaled_gap, axis=1).reshape(rows_dev, cols_dev)
    return jnp.where(valid == 1, jnp.minimum(prev_dist, nearest), jnp.float32(0.0))


def solution(mesh):
    return jax.shard_map(
        shards,
        mesh=mesh,
        in_specs=(P("rows", "cols", None), P(), P("rows", "cols"), P("rows", "cols"), P(), P()),
        out_specs=P("rows", "cols"),
        check_vma=False,
    )
```

profile of v0, /device:TPU:2, one launch (start us, length us, event | category | flops | bytes accessed | tf_op | source)
XLA Modules:
  0.0 382.1 jit_solution(17740806826330092399)
XLA Ops:
  6.5 0.0 copy-start
  6.5 0.0 all-reduce.2.cloned.1.call-start
  6.5 1.2 fusion.6
  7.8 1.9 collective-permute-start
  9.7 3.6 collective-permute-start.1
  13.3 0.7 broadcast_compare_fusion
  14.0 0.7 compare_select_fusion
  14.7 2.1 collective-permute-done
  16.9 6.7 %constant_dynamic-update-slice_fusion.1 = bf16[34,128,1536]{2,1,0:T(8,128)(2,1)S(1)} fusion(bf16[34,128,1536]{2,1,0:T(8,128)(2,1)S(1)} %constant_dynamic-update-slice_fusion.2, bf16[32,128,1536]{2,1,0:T(8,128)(2,1)} %param.6), kind=kLoop, calls=%fused_computation.25 | loop fusion | bytes 25165824
  23.6 0.0 collective-permute-done.1
  23.6 0.0 copy-start.1
  23.6 4.8 %copy-done.1 = bf16[34,128,1536]{2,1,0:T(8,128)(2,1)} copy-done((bf16[34,128,1536]{2,1,0:T(8,128)(2,1)}, bf16[34,128,1536]{2,1,0:T(8,128)(2,1)S(1)}, u32[]{:S(2)}) %copy-start.1) | copy-done | bytes 13369368
  28.5 0.3 fusion.5
  28.8 3.8 %collective-permute-start.2 = (bf16[34,1,1536]{2,0,1:T(8,128)(2,1)S(1)}, bf16[34,1,1536]{2,0,1:T(8,128)(2,1)S(1)}, u32[]{:S(2)}, u32[]{:S(2)}) collective-permute-start(bf16[34,1,1536]{2,0,1:T(8,128)(2,1)S(1)} %copy.15), channel_id=1, source_target_pairs={{0,1},{1,2},{2,3},{3,4},{4,5},{5,6},{6,7},{7,8},{8,9},{9,10},{10,1... | collective-permute-start | bytes 313352 | tf_op jit(solution)/shard_map/ppermute | solution.py:14
  32.7 1.3 collective-permute-start.3
  34.0 1.1 collective-permute-done.2
  35.1 0.2 copy.16
  35.2 4.2 %collective-permute-done.3 = bf16[34,1,1536]{2,0,1:T(8,128)(2,1)S(1)} collective-permute-done((bf16[34,1,1536]{2,0,1:T(8,128)(2,1)S(1)}, bf16[34,1,1536]{2,0,1:T(8,128)(2,1)S(1)}, u32[]{:S(2)}, u32[]{:S(2)}) %collective-permute-start.3) | collective-permute-done | bytes 104480 | tf_op jit(solution)/shard_map/ppermute | solution.py:17
  39.5 0.2 copy.18
  39.6 47.2 %add_multiply_fusion = f32[32,128,1536]{2,1,0:T(8,128)} fusion(bf16[32,128,1536]{2,1,0:T(8,128)(2,1)} %param.6, bf16[34,128,1536]{2,1,0:T(8,128)(2,1)} %copy-done.1, bf16[34,1,1536]{2,1,0:T(2,128)(2,1)S(1)} %copy.18, bf16[34,1,1536]{2,1,0:T(2,128)(2,1)S(1)} %copy.16, bf16[1,128,1536]{2,1,0:T(8,128)(2,1)S(1)} %collective-permute-done.1, ...), kind=kLoop, calls=%fused_computation.1 | loop fusion | flops 264241152 | bytes 52113408 | tf_op jit(solution)/shard_map/div | solution.py:29
  86.8 0.0 copy-done
  86.9 18.7 %multiply_reduce_fusion.1 = (f32[4096]{0:T(1024)S(1)}, f32[4096,128]{0,1:T(8,128)S(1)}) fusion(f32[4096,1536]{1,0:T(8,128)} %bitcast.9, bf16[1536,128]{1,0:T(8,128)(2,1)S(1)} %copy-done), kind=kOutput, calls=%fused_computation.19 | convolution fusion | flops 9664720896 | bytes 27672576 | tf_op jit(solution)/shard_map/dot_general | solution.py:39
  105.6 0.0 copy-start.2
  105.6 0.0 copy-start.3
  105.6 1.9 copy.19
  107.5 2.6 gather_fusion
  110.1 0.8 broadcast_select_fusion
  111.0 0.0 all-reduce.2.cloned.1.call-update
  111.0 253.3 %all-reduce.2.cloned.1.call-done = f32[512,128]{1,0:T(8,128)} async-done(((f32[512,128]{1,0:T(8,128)}), f32[512,128]{1,0:T(8,128)}) %all-reduce.2.cloned.1.call-update) | async-done | bytes 262160 | tf_op jit(solution)/shard_map/psum | solution.py:41
  364.3 1.1 multiply_reduce_fusion.2
  365.4 9.2 %multiply_reduce_fusion = f32[4096]{0:T(1024)S(1)} fusion(f32[4096,128]{0,1:T(8,128)S(1)} %get-tuple-element.10, f32[512,128]{1,0:T(8,128)} %all-reduce.2.cloned.1.call-done, f32[512]{0:T(512)S(1)} %multiply_reduce_fusion.2, f32[4096]{0:T(1024)S(1)} %get-tuple-element.9), kind=kOutput, calls=%fused_computation.18 | convolution fusion | flops 3231707136 | bytes 2394112 | tf_op jit(solution)/shard_map/dot_general | solution.py:44
  374.6 0.0 copy-done.2
  374.6 0.0 copy-done.3
  374.7 0.6 fusion.4
  (5 shorter events, 0.1 us)
Async XLA Ops:
  6.5 80.3 %copy-start = (bf16[1536,128]{1,0:T(8,128)(2,1)S(1)}, bf16[1536,128]{1,0:T(8,128)(2,1)}, u32[]{:S(2)}) copy-start(bf16[1536,128]{1,0:T(8,128)(2,1)} %param.7) | copy-start | bytes 1179652
  6.5 357.8 %all-reduce.2.cloned.1.call-start = ((), (), s32[]{:S(2)}) async-start(), calls=%async_computation | async-start | bytes 524288 | tf_op jit(solution)/shard_map/psum | solution.py:41
  7.8 9.1 %collective-permute-start = (bf16[1,128,1536]{2,1,0:T(8,128)(2,1)S(1)}, bf16[1,128,1536]{2,1,0:T(8,128)(2,1)S(1)}, u32[]{:S(2)}, u32[]{:S(2)}) collective-permute-start(bf16[1,128,1536]{2,1,0:T(8,128)(2,1)S(1)} %get-tuple-element.8), channel_id=1, source_target_pairs={{0,32},{32,64},{64,96},{96,128},{128,160},{160,192},{192,224},{1,3... | collective-permute-start | bytes 1179656 | tf_op jit(solution)/shard_map/ppermute | solution.py:14
  9.7 13.9 %collective-permute-start.1 = (bf16[1,128,1536]{2,1,0:T(8,128)(2,1)S(1)}, bf16[1,128,1536]{2,1,0:T(8,128)(2,1)S(1)}, u32[]{:S(2)}, u32[]{:S(2)}) collective-permute-start(bf16[1,128,1536]{2,1,0:T(8,128)(2,1)S(1)} %get-tuple-element.7), channel_id=1, source_target_pairs={{32,0},{64,32},{96,64},{128,96},{160,128},{192,160},{224,192},{33,... | collective-permute-start | bytes 1179656 | tf_op jit(solution)/shard_map/ppermute | solution.py:17
  23.6 4.8 %copy-start.1 = (bf16[34,128,1536]{2,1,0:T(8,128)(2,1)}, bf16[34,128,1536]{2,1,0:T(8,128)(2,1)S(1)}, u32[]{:S(2)}) copy-start(bf16[34,128,1536]{2,1,0:T(8,128)(2,1)S(1)} %constant_dynamic-update-slice_fusion) | copy-start | bytes 40108036
  28.8 6.3 %collective-permute-start.2 = (bf16[34,1,1536]{2,0,1:T(8,128)(2,1)S(1)}, bf16[34,1,1536]{2,0,1:T(8,128)(2,1)S(1)}, u32[]{:S(2)}, u32[]{:S(2)}) collective-permute-start(bf16[34,1,1536]{2,0,1:T(8,128)(2,1)S(1)} %copy.15), channel_id=1, source_target_pairs={{0,1},{1,2},{2,3},{3,4},{4,5},{5,6},{6,7},{7,8},{8,9},{9,10},{10,1... | collective-permute-start | bytes 313352 | tf_op jit(solution)/shard_map/ppermute | solution.py:14
  32.7 6.8 %collective-permute-start.3 = (bf16[34,1,1536]{2,0,1:T(8,128)(2,1)S(1)}, bf16[34,1,1536]{2,0,1:T(8,128)(2,1)S(1)}, u32[]{:S(2)}, u32[]{:S(2)}) collective-permute-start(bf16[34,1,1536]{2,0,1:T(8,128)(2,1)S(1)} %copy.17), channel_id=1, source_target_pairs={{1,0},{2,1},{3,2},{4,3},{5,4},{6,5},{7,6},{8,7},{9,8},{10,9},{11,1... | collective-permute-start | bytes 313352 | tf_op jit(solution)/shard_map/ppermute | solution.py:17
  105.6 269.0 %copy-start.2 = (f32[32,128]{1,0:T(8,128)S(1)}, f32[32,128]{1,0:T(8,128)}, u32[]{:S(2)}) copy-start(f32[32,128]{1,0:T(8,128)} %param.8) | copy-start | bytes 49156
  105.6 269.0 %copy-start.3 = (s32[32,128]{1,0:T(8,128)S(1)}, s32[32,128]{1,0:T(8,128)}, u32[]{:S(2)}) copy-start(s32[32,128]{1,0:T(8,128)} %param.9) | copy-start | bytes 49156
Sparse Core Ops, SparseCore 0:
  111.1 253.1 all-reduce.1
where the time goes:
time: 382 us
  waiting for transfers between devices  261 us (68%)
  other arithmetic  51.2 us (13%)
  matrix products  27.9 us (7%)
  local copies, waits for them, and re-layouts  18 us (5%)
  between operations  13.6 us (4%)
  starting transfers between devices  10.7 us (3%)
    psum x1, waiting for transfers between devices, shards(): pick_rows = lax.psum(local_rows, ('rows', 'cols'))  253 us
    div x1, other arithmetic, window_sum(): return total / 9.0  47.2 us
    dot_general x1, matrix products, shards(): projected = jnp.dot(pooled, proj_full, precision=lax.Precision.HIGHEST)  18.7 us
    unnamed x10, local copies, waits for them, and re-layouts  11.6 us
    dot_general x1, matrix products, shards(): jnp.dot(projected, pick_rows.T, precision=lax.Precision.HIGHEST)  9.21 us
  transfers between devices with their start and end apart: 5, of which 4 were waited for; matrix products, arithmetic and copies ran while one was open for 2% of the time, Pallas kernels for 0%

commit v1 on v0

--- a/solution.py
+++ b/solution.py
@@ -38,7 +38,7 @@
     pooled = window_sum(padded, rows_dev, cols_dev).reshape(rows_dev * cols_dev, channels)
     projected = jnp.dot(pooled, proj_full, precision=lax.Precision.HIGHEST)
     local_rows = jnp.where(owned[:, None], projected[pick_slot], jnp.float32(0.0))
-    pick_rows = lax.psum(local_rows, ("rows", "cols"))
+    pick_rows = jnp.sum(lax.all_gather(local_rows, ("rows", "cols")), axis=0)
     pick_sq = jnp.sum(pick_rows * pick_rows, axis=1)
     own_sq = jnp.sum(projected * projected, axis=1)
     inner_prod = jnp.dot(projected, pick_rows.T, precision=lax.Precision.HIGHEST)

time: 382 us -> 366 us (0.958)
  waiting for transfers between devices: 261 us -> 225 us
  other arithmetic: 51.2 us -> 71.2 us
    psum x1 -> x0, waiting for transfers between devices: 253 us -> none  [shards(): pick_rows = lax.psum(local_rows, ('rows', 'cols'))]
    all_gather x0 -> x1, waiting for transfers between devices: none -> 217 us  [shards(): pick_rows = jnp.sum(lax.all_gather(local_rows, ('rows', 'cols')), axis=0)]
    reduce_sum x0 -> x1, other arithmetic: none -> 21 us  [shards(): pick_rows = jnp.sum(lax.all_gather(local_rows, ('rows', 'cols')), axis=0)]
    ppermute x2, waiting for transfers between devices: 3.22 us -> 7.28 us  [padded_2(): lax.ppermute(lax.slice_in_dim(block, block.shape[dim] - width, None, axis...]
where the time goes in v1:
time: 366 us; the launch traced here: 365 us
  waiting for transfers between devices  225 us (61%)
  other arithmetic  71.2 us (19%)
  matrix products  26.9 us (7%)
  local copies, waits for them, and re-layouts  18 us (5%)
  between operations  13.6 us (4%)
  starting transfers between devices  10.2 us (3%)
    all_gather x1, waiting for transfers between devices, shards(): pick_rows = jnp.sum(lax.all_gather(local_rows, ('rows', 'cols')), axis=0)  217 us
    div x1, other arithmetic, window_sum(): return total / 9.0  47.2 us
    reduce_sum x1, other arithmetic, shards(): pick_rows = jnp.sum(lax.all_gather(local_rows, ('rows', 'cols')), axis=0)  21 us
    dot_general x1, matrix products, shards(): projected = jnp.dot(pooled, proj_full, precision=lax.Precision.HIGHEST)  18.7 us
    unnamed x10, local copies, waits for them, and re-layouts  11.6 us
    dot_general x1, matrix products, shards(): jnp.dot(projected, pick_rows.T, precision=lax.Precision.HIGHEST)  8.2 us
  transfers between devices with their start and end apart: 5, of which 4 were waited for; matrix products, arithmetic and copies ran while one was open for 2% of the time, Pallas kernels for 0%

profile of v1, /device:TPU:2, one launch (start us, length us, event | category | flops | bytes accessed | tf_op | source)
XLA Modules:
  0.0 364.8 jit_solution(11232785804806109961)
XLA Ops:
  6.5 0.0 copy-start
  6.5 0.0 all-gather.2.cloned.1.call-start
  6.5 1.2 fusion.6
  7.8 1.9 collective-permute-start.1
  9.7 2.4 collective-permute-start
  12.1 0.7 broadcast_compare_fusion
  12.8 0.7 compare_select_fusion
  13.5 5.9 %collective-permute-done = bf16[1,128,1536]{2,1,0:T(8,128)(2,1)S(1)} collective-permute-done((bf16[1,128,1536]{2,1,0:T(8,128)(2,1)S(1)}, bf16[1,128,1536]{2,1,0:T(8,128)(2,1)S(1)}, u32[]{:S(2)}, u32[]{:S(2)}) %collective-permute-start) | collective-permute-done | bytes 393248 | tf_op jit(solution)/shard_map/ppermute | solution.py:14
  19.5 6.7 %constant_dynamic-update-slice_fusion.1 = bf16[34,128,1536]{2,1,0:T(8,128)(2,1)S(1)} fusion(bf16[34,128,1536]{2,1,0:T(8,128)(2,1)S(1)} %constant_dynamic-update-slice_fusion.2, bf16[32,128,1536]{2,1,0:T(8,128)(2,1)} %param.6), kind=kLoop, calls=%fused_computation.25 | loop fusion | bytes 25165824
  26.1 0.0 collective-permute-done.1
  26.2 0.0 copy-start.1
  26.2 4.8 %copy-done.1 = bf16[34,128,1536]{2,1,0:T(8,128)(2,1)} copy-done((bf16[34,128,1536]{2,1,0:T(8,128)(2,1)}, bf16[34,128,1536]{2,1,0:T(8,128)(2,1)S(1)}, u32[]{:S(2)}) %copy-start.1) | copy-done | bytes 13369368
  31.0 0.3 fusion.5
  31.4 1.3 collective-permute-start.3
  32.7 4.6 %collective-permute-start.2 = (bf16[34,1,1536]{2,0,1:T(8,128)(2,1)S(1)}, bf16[34,1,1536]{2,0,1:T(8,128)(2,1)S(1)}, u32[]{:S(2)}, u32[]{:S(2)}) collective-permute-start(bf16[34,1,1536]{2,0,1:T(8,128)(2,1)S(1)} %copy.20), channel_id=1, source_target_pairs={{0,1},{1,2},{2,3},{3,4},{4,5},{5,6},{6,7},{7,8},{8,9},{9,10},{10,1... | collective-permute-start | bytes 313352 | tf_op jit(solution)/shard_map/ppermute | solution.py:14
  37.3 0.9 collective-permute-done.3
  38.2 0.2 copy.23
  38.4 1.3 collective-permute-done.2
  39.7 0.2 copy.21
  39.9 47.2 %add_multiply_fusion = f32[32,128,1536]{2,1,0:T(8,128)} fusion(bf16[32,128,1536]{2,1,0:T(8,128)(2,1)} %param.6, bf16[34,128,1536]{2,1,0:T(8,128)(2,1)} %copy-done.1, bf16[34,1,1536]{2,1,0:T(2,128)(2,1)S(1)} %copy.23, bf16[34,1,1536]{2,1,0:T(2,128)(2,1)S(1)} %copy.21, bf16[1,128,1536]{2,1,0:T(8,128)(2,1)S(1)} %collective-permute-done.1, ...), kind=kLoop, calls=%fused_computation.1 | loop fusion | flops 264241152 | bytes 52113408 | tf_op jit(solution)/shard_map/div | solution.py:29
  87.1 0.0 copy-done
  87.1 18.7 %multiply_reduce_fusion.1 = (f32[4096]{0:T(1024)S(1)}, f32[4096,128]{0,1:T(8,128)S(1)}) fusion(f32[4096,1536]{1,0:T(8,128)} %bitcast.11, bf16[1536,128]{1,0:T(8,128)(2,1)S(1)} %copy-done), kind=kOutput, calls=%fused_computation.19 | convolution fusion | flops 9664720896 | bytes 27672576 | tf_op jit(solution)/shard_map/dot_general | solution.py:39
  105.9 1.9 copy.24
  107.7 2.6 gather_fusion
  110.3 0.8 bitcast_select_fusion
  111.2 0.0 all-gather.2.cloned.1.call-update
  111.2 0.0 copy-start.2
  111.2 0.0 copy-start.3
  111.2 216.7 %all-gather.2.cloned.1.call-done = f32[256,512,128]{2,1,0:T(8,128)} async-done(((f32[1,512,128]{2,1,0:T(8,128)}), f32[256,512,128]{2,1,0:T(8,128)}) %all-gather.2.cloned.1.call-update) | async-done | bytes 67108880 | tf_op jit(solution)/shard_map/all_gather | solution.py:41
  327.9 21.0 %reduce_sum.28 = f32[512,128]{1,0:T(8,128)S(1)} reduce(f32[256,512,128]{2,1,0:T(8,128)} %all-gather.2.cloned.1.call-done, f32[]{:T(128)} %constant.7.clone.1), dimensions={0}, to_apply=%region_1.2 | reduce | flops 16711680 | bytes 67371008 | tf_op jit(solution)/shard_map/reduce_sum | solution.py:41
  349.0 0.1 multiply_reduce_fusion.2
  349.1 8.2 %multiply_reduce_fusion = f32[4096]{0:T(1024)S(1)} fusion(f32[4096,128]{0,1:T(8,128)S(1)} %get-tuple-element.10, f32[512,128]{1,0:T(8,128)S(1)} %reduce_sum.28, f32[512]{0:T(512)S(1)} %multiply_reduce_fusion.2, f32[4096]{0:T(1024)S(1)} %get-tuple-element.9), kind=kOutput, calls=%fused_computation.18 | convolution fusion | flops 3231707136 | bytes 2394112 | tf_op jit(solution)/shard_map/dot_general | solution.py:44
  357.3 0.0 copy-done.2
  357.3 0.0 copy-done.3
  357.4 0.6 fusion.4
  (5 shorter events, 0.1 us)
Async XLA Ops:
  6.5 80.6 %copy-start = (bf16[1536,128]{1,0:T(8,128)(2,1)S(1)}, bf16[1536,128]{1,0:T(8,128)(2,1)}, u32[]{:S(2)}) copy-start(bf16[1536,128]{1,0:T(8,128)(2,1)} %param.7) | copy-start | bytes 1179652
  6.5 321.4 %all-gather.2.cloned.1.call-start = ((), (), s32[]{:S(2)}) async-start(), calls=%async_computation | async-start | bytes 67371008 | tf_op jit(solution)/shard_map/all_gather | solution.py:41
  7.8 18.4 %collective-permute-start.1 = (bf16[1,128,1536]{2,1,0:T(8,128)(2,1)S(1)}, bf16[1,128,1536]{2,1,0:T(8,128)(2,1)S(1)}, u32[]{:S(2)}, u32[]{:S(2)}) collective-permute-start(bf16[1,128,1536]{2,1,0:T(8,128)(2,1)S(1)} %get-tuple-element.7), channel_id=1, source_target_pairs={{32,0},{64,32},{96,64},{128,96},{160,128},{192,160},{224,192},{33,... | collective-permute-start | bytes 1179656 | tf_op jit(solution)/shard_map/ppermute | solution.py:17
  9.7 9.7 %collective-permute-start = (bf16[1,128,1536]{2,1,0:T(8,128)(2,1)S(1)}, bf16[1,128,1536]{2,1,0:T(8,128)(2,1)S(1)}, u32[]{:S(2)}, u32[]{:S(2)}) collective-permute-start(bf16[1,128,1536]{2,1,0:T(8,128)(2,1)S(1)} %get-tuple-element.8), channel_id=1, source_target_pairs={{0,32},{32,64},{64,96},{96,128},{128,160},{160,192},{192,224},{1,3... | collective-permute-start | bytes 1179656 | tf_op jit(solution)/shard_map/ppermute | solution.py:14
  26.2 4.8 %copy-start.1 = (bf16[34,128,1536]{2,1,0:T(8,128)(2,1)}, bf16[34,128,1536]{2,1,0:T(8,128)(2,1)S(1)}, u32[]{:S(2)}) copy-start(bf16[34,128,1536]{2,1,0:T(8,128)(2,1)S(1)} %constant_dynamic-update-slice_fusion) | copy-start | bytes 40108036
  31.4 6.8 %collective-permute-start.3 = (bf16[34,1,1536]{2,0,1:T(8,128)(2,1)S(1)}, bf16[34,1,1536]{2,0,1:T(8,128)(2,1)S(1)}, u32[]{:S(2)}, u32[]{:S(2)}) collective-permute-start(bf16[34,1,1536]{2,0,1:T(8,128)(2,1)S(1)} %copy.22), channel_id=1, source_target_pairs={{1,0},{2,1},{3,2},{4,3},{5,4},{6,5},{7,6},{8,7},{9,8},{10,9},{11,1... | collective-permute-start | bytes 313352 | tf_op jit(solution)/shard_map/ppermute | solution.py:17
  32.7 7.0 %collective-permute-start.2 = (bf16[34,1,1536]{2,0,1:T(8,128)(2,1)S(1)}, bf16[34,1,1536]{2,0,1:T(8,128)(2,1)S(1)}, u32[]{:S(2)}, u32[]{:S(2)}) collective-permute-start(bf16[34,1,1536]{2,0,1:T(8,128)(2,1)S(1)} %copy.20), channel_id=1, source_target_pairs={{0,1},{1,2},{2,3},{3,4},{4,5},{5,6},{6,7},{7,8},{8,9},{9,10},{10,1... | collective-permute-start | bytes 313352 | tf_op jit(solution)/shard_map/ppermute | solution.py:14
  111.2 246.1 %copy-start.2 = (f32[32,128]{1,0:T(8,128)S(1)}, f32[32,128]{1,0:T(8,128)}, u32[]{:S(2)}) copy-start(f32[32,128]{1,0:T(8,128)} %param.8) | copy-start | bytes 49156
  111.2 246.1 %copy-start.3 = (s32[32,128]{1,0:T(8,128)S(1)}, s32[32,128]{1,0:T(8,128)}, u32[]{:S(2)}) copy-start(s32[32,128]{1,0:T(8,128)} %param.9) | copy-start | bytes 49156
Sparse Core Ops, SparseCore 0:
  111.3 216.5 all-gather.1
